TPU v7x, 32 devices: a whole 2x2x4 slice. The times are simulated.
32 devices in a mesh: dp: 8 (over y, x, core), tensor: 4 (over z).
Axes of the slice: x: 2, y: 2, z: 4, core: 2. Of those that a mesh axis runs over, the one named last changes fastest.
Arguments:
- text: bfloat16 [8192, 768], P(('dp', 'tensor')), may hold values from -6 to 6
- image: bfloat16 [2304, 1024], P(('dp', 'tensor')), may hold values from -6 to 6
- text_segment: int32 [64, 128], P('dp'), may hold values from 0 to 3, as said below
- image_segment: int32 [64, 36], P('dp'), may hold values from 0 to 3, as said below
- text_cross_weight: bfloat16 [768, 3, 1024], P(None, None, 'tensor'), may hold values from -0.21875 to 0.21875
- text_cross_bias: bfloat16 [2, 1024], P(None, 'tensor'), may hold values from -3 to 3
- text_cross_output: bfloat16 [1024, 768], P('tensor'), may hold values from -0.5 to 0.5
- text_inner_expand: bfloat16 [768, 3072], P(None, 'tensor'), may hold values from -0.21875 to 0.21875
- text_inner_offset: bfloat16 [3072], P('tensor'), may hold values from -3 to 3
- text_inner_reduce: bfloat16 [3072, 768], P('tensor'), may hold values from -0.15625 to 0.15625
- text_self_weight: bfloat16 [768, 3, 768], P(None, None, 'tensor'), may hold values from -0.21875 to 0.21875
- text_self_bias: bfloat16 [2, 768], P(None, 'tensor'), may hold values from -3 to 3
- text_self_output: bfloat16 [768, 768], P('tensor'), may hold values from -1.25 to 1.25
- text_outer_expand: bfloat16 [768, 3072], P(None, 'tensor'), may hold values from -0.21875 to 0.21875
- text_outer_offset: bfloat16 [3072], P('tensor'), may hold values from -3 to 3
- text_outer_reduce: bfloat16 [3072, 768], P('tensor'), may hold values from -0.15625 to 0.15625
- text_branch_bias: bfloat16 [4, 768], replicated, may hold values from -2 to 2
- text_norm_gain: bfloat16 [4, 768], replicated, may hold values from 0.099609375 to 1.8984375
- text_norm_shift: bfloat16 [4, 768], replicated, may hold values from -2 to 2
- image_cross_weight: bfloat16 [1024, 3, 1024], P(None, None, 'tensor'), may hold values from -0.1875 to 0.1875
- image_cross_bias: bfloat16 [2, 1024], P(None, 'tensor'), may hold values from -3 to 3
- image_cross_output: bfloat16 [1024, 1024], P('tensor'), may hold values from -1 to 1
- image_inner_expand: bfloat16 [1024, 1024], P(None, 'tensor'), may hold values from -0.1875 to 0.1875
- image_inner_offset: bfloat16 [1024], P('tensor'), may hold values from -3 to 3
- image_inner_reduce: bfloat16 [1024, 1024], P('tensor'), may hold values from -0.25 to 0.25
- image_self_weight: bfloat16 [1024, 3, 1024], P(None, None, 'tensor'), may hold values from -0.1875 to 0.1875
- image_self_bias: bfloat16 [2, 1024], P(None, 'tensor'), may hold values from -3 to 3
- image_self_output: bfloat16 [1024, 1024], P('tensor'), may hold values from -0.5 to 0.5
- image_outer_expand: bfloat16 [1024, 1024], P(None, 'tensor'), may hold values from -0.1875 to 0.1875
- image_outer_offset: bfloat16 [1024], P('tensor'), may hold values from -3 to 3
- image_outer_reduce: bfloat16 [1024, 1024], P('tensor'), may hold values from -0.25 to 0.25
- image_branch_bias: bfloat16 [4, 1024], replicated, may hold values from -2 to 2
- image_norm_gain: bfloat16 [4, 1024], replicated, may hold values from 0.099609375 to 1.8984375
- image_norm_shift: bfloat16 [4, 1024], replicated, may hold values from -2 to 2
- text_cotangent: bfloat16 [8192, 768], P(('dp', 'tensor')), may hold values from -6 to 6
- image_cotangent: bfloat16 [2304, 1024], P(('dp', 'tensor')), may hold values from -6 to 6
Outputs:
- text_result: float32 [8192, 768], P(('dp', 'tensor'))
- image_result: float32 [2304, 1024], P(('dp', 'tensor'))
- delta_text: float32 [8192, 768], P(('dp', 'tensor'))
- delta_image: float32 [2304, 1024], P(('dp', 'tensor'))
- delta_text_cross_weight: float32 [768, 3, 1024], P('dp', None, 'tensor')
- delta_text_cross_bias: float32 [2, 1024], P(None, 'tensor')
- delta_text_cross_output: float32 [1024, 768], P('tensor', 'dp')
- delta_text_inner_expand: float32 [768, 3072], P('dp', 'tensor')
- delta_text_inner_offset: float32 [3072], P('tensor')
- delta_text_inner_reduce: float32 [3072, 768], P('tensor', 'dp')
- delta_text_self_weight: float32 [768, 3, 768], P('dp', None, 'tensor')
- delta_text_self_bias: float32 [2, 768], P(None, 'tensor')
- delta_text_self_output: float32 [768, 768], P('tensor', 'dp')
- delta_text_outer_expand: float32 [768, 3072], P('dp', 'tensor')
- delta_text_outer_offset: float32 [3072], P('tensor')
- delta_text_outer_reduce: float32 [3072, 768], P('tensor', 'dp')
- delta_text_branch_bias: float32 [4, 768], replicated
- delta_text_norm_gain: float32 [4, 768], replicated
- delta_text_norm_shift: float32 [4, 768], replicated
- delta_image_cross_weight: float32 [1024, 3, 1024], P('dp', None, 'tensor')
- delta_image_cross_bias: float32 [2, 1024], P(None, 'tensor')
- delta_image_cross_output: float32 [1024, 1024], P('tensor', 'dp')
- delta_image_inner_expand: float32 [1024, 1024], P('dp', 'tensor')
- delta_image_inner_offset: float32 [1024], P('tensor')
- delta_image_inner_reduce: float32 [1024, 1024], P('tensor', 'dp')
- delta_image_self_weight: float32 [1024, 3, 1024], P('dp', None, 'tensor')
- delta_image_self_bias: float32 [2, 1024], P(None, 'tensor')
- delta_image_self_output: float32 [1024, 1024], P('tensor', 'dp')
- delta_image_outer_expand: float32 [1024, 1024], P('dp', 'tensor')
- delta_image_outer_offset: float32 [1024], P('tensor')
- delta_image_outer_reduce: float32 [1024, 1024], P('tensor', 'dp')
- delta_image_branch_bias: float32 [4, 1024], replicated
- delta_image_norm_gain: float32 [4, 1024], replicated
- delta_image_norm_shift: float32 [4, 1024], replicated
Inputs may be any that keep to these rules, and one draw needn't show every extreme that they name: `text_segment`: along each row the caption numbers never fall and every number 0 to 3 appears in every row. `image_segment`: along each row the image numbers never fall and every number 0 to 3 appears in every row.
All inputs are finite; a program needn't handle non-finite values.
Results may differ from a plain program's by a relative error of at most 0.035.
Values may be sent and summed in bfloat16 or wider, within the bound.
A program may use at most 192 MiB of HBM per device.

v0:
```python
import functools
import math

import jax
import jax.numpy as jnp
from jax import lax
from jax.experimental import pallas as pl
from jax.experimental.pallas import tpu as pltpu
from jax.sharding import PartitionSpec as P

CO_DH = 128
TS_DH = 64
VS_DH = 128
LANES = 256
MESH = pl.DeviceIdType.MESH

norm_eps = 1e-05
root_half = 0.7071067811865476
inv_root_tau = 0.3989422804014327
f32 = jnp.float32
bf16 = jnp.bfloat16


def gelu_value(hidden):
    return 0.5 * hidden * (1.0 + lax.erf(hidden * root_half))


def gelu_slope(hidden):
    return (
        0.5 * (1.0 + lax.erf(hidden * root_half))
        + hidden * jnp.exp(-0.5 * hidden * hidden) * inv_root_tau
    )


def norm_forward(hidden, gain, shift):
    center = hidden - jnp.mean(hidden, axis=1, keepdims=True)
    scale = lax.rsqrt(jnp.mean(center * center, axis=1, keepdims=True) + norm_eps)
    normed = center * scale
    return normed * gain + shift, normed, scale


def norm_backward(upstream, normed, scale, gain):
    inner = upstream * gain
    return scale * (
        inner
        - jnp.mean(inner, axis=1, keepdims=True)
        - normed * jnp.mean(inner * normed, axis=1, keepdims=True)
    )


def times(left, right):
    return jnp.dot(left, right, preferred_element_type=f32)


def times_transpose(left, right):
    return lax.dot_general(left, right, (((1,), (1,)), ((), ())), preferred_element_type=f32)


def outer_sum(left, right):
    return lax.dot_general(left, right, (((0,), (0,)), ((), ())), preferred_element_type=f32)


def swap(value, axis, mask):
    return lax.ppermute(value, axis, [(i, i ^ mask) for i in range(lax.axis_size(axis))])


def segments_of(mats):
    dp, found = lax.axis_size("dp"), []
    for index, (_, parts) in enumerate(mats):
        base = 0
        for total in parts:
            found.append((index, base, total // dp))
            base += total
    return found


def greet(partners):
    barrier = pltpu.get_barrier_semaphore()
    for partner in partners:
        pl.semaphore_signal(barrier, inc=1, device_id=partner, device_id_type=MESH)
    pl.semaphore_wait(barrier, len(partners))


EARLY = (((0, 1), (2, 3)), ((4, 5), (6, 7)), ((8, 8), (9, 10)))
FIRST_TASK = (6, 10, 14)


def early_columns(text_width, image_width, text_hidden, image_hidden, text_own, image_own):
    counts = [text_width, image_width, text_hidden, image_hidden, text_own, image_own]
    counts += [text_hidden, image_hidden]
    found, at = [], 0
    for count in counts:
        found.append((at, count))
        at += count
    return found


def early_outs(jobs, widths, states):
    outs = []
    for stage in range(3):
        for k, state in enumerate(states):
            tokens, width = state.shape
            if stage == 1:
                shapes = [((tokens, 4 * widths[2 + k]), f32), ((tokens, 4 * widths[2 + k]), bf16)]
            else:
                _, _, size, heads, shift = jobs[stage // 2][k]
                columns = (shift or 3 * size * heads) + (size * heads if shift else 0)
                shapes = [((tokens, 4 * columns), bf16), ((tokens, 4 * (shift + size * heads)), bf16)]
            shapes += [((tokens, width), f32), ((tokens, width), f32), ((tokens, 128), f32)]
            outs += shapes
    return outs


def gather_kernel(segments, stage_of, n_mats, jobs, places, shapes, *refs):
    n_in = n_mats + 1
    locals_, refs = refs[:n_in], refs[n_in:]
    states, rows, ids, refs = refs[:2], refs[2:8], refs[8:12], refs[12:]
    outs, refs = refs[:n_in], refs[n_in:]
    results, refs = refs[: len(shapes)], refs[len(shapes) :]
    values, refs = refs[: len(shapes)], refs[len(shapes) :]
    blocks, bias, (send_sems, recv_sems, local_sems) = refs[:4], refs[4], refs[5:]
    me, place_t = lax.axis_index("dp"), lax.axis_index("tensor")
    lines = [{"tensor": jnp.bitwise_xor(place_t, s)} for s in range(1, 4)]
    core, across, along = [{"dp": jnp.bitwise_xor(me, mask)} for mask in (1, 2, 4)]
    greet(lines + [core, across, along])
    copies, moves = [], []

    def copy(source, target, device):
        k = len(copies)
        item = pltpu.make_async_remote_copy(
            source, target, send_sems.at[k], recv_sems.at[k], device_id=device, device_id_type=MESH
        )
        item.start()
        copies.append(item)
        return item

    def move(source, target):
        item = pltpu.make_async_copy(source, target, local_sems.at[len(moves)])
        item.start()
        moves.append(item)
        return item

    def rows_of(segment, mask):
        _, base, count = segment
        return pl.ds(pl.multiple_of(base + jnp.bitwise_xor(me, mask) * count, 8), count)

    def pass_on(segment, mask, device, low=0, high=1):
        index = segment[0]
        width = outs[index].shape[2] // 2
        part = outs[index].at[
            pl.ds(1, 3), rows_of(segment, mask), pl.ds(low * width, (high + 1 - low) * width)
        ]
        return copy(part, part, device)

    late = [[] for _ in range(4)]
    bias_copies = [copy(locals_[-1], outs[-1].at[s], lines[s]) for s in range(3)]
    arrivals = []
    for segment in segments:
        index, part = segment[0], rows_of(segment, 0)
        arrivals.append(
            [copy(locals_[index].at[part], outs[index].at[s + 1, part], lines[s]) for s in range(3)]
        )
    for index in range(n_mats):
        late[stage_of[index]].append(copy(locals_[index], outs[index].at[0], core))

    loads, finished = {}, []
    values_of = [
        [values[(2 * stage + k) * 5 : (2 * stage + k + 1) * 5] for k in range(2)] for stage in range(3)
    ]

    def load(stage, s):
        slot, items = s % 2, []
        for k in range(2):
            for part in range(2):
                if part and EARLY[stage][k][0] == EARLY[stage][k][1]:
                    continue
                source = outs[EARLY[stage][k][part]]
                items.append(
                    move(source.at[s], blocks[2 * k + part].at[slot, pl.ds(0, source.shape[1])])
                )
        loads[stage, s] = items

    def run(stage, s):
        if s == 0:
            for item in late[stage]:
                item.wait_recv()
            if stage == 0:
                for item in bias_copies:
                    item.wait_recv()
                for item in [move(locals_[-1], bias.at[0]), move(outs[-1], bias.at[pl.ds(1, 3)])]:
                    item.wait()
            load(stage, 0)
        for item in loads[stage, s]:
            item.wait()
        if s < 3:
            load(stage, s + 1)
        streams = []
        for k in range(2):
            first, second = EARLY[stage][k]
            weight = blocks[2 * k].at[s % 2, pl.ds(0, outs[first].shape[1])]
            output = blocks[2 * k + 1].at[s % 2, pl.ds(0, outs[second].shape[1])]
            if first == second:
                output = weight
            at, count = places[2 * stage + k]
            offset = bias.at[s, :, pl.ds(at, count)]
            state = states[k] if stage == 0 else values_of[stage - 1][k][2]
            mine = values_of[stage][k]
            cut = [
                item.at[:, pl.ds(s * (item.shape[1] // 4), item.shape[1] // 4)] for item in mine[:2]
            ]
            ins = (state, weight, output, offset, rows[2 * stage + k])
            streams.append((ins, [*cut, *mine[2:]]))
        Step.now = s
        if stage == 1:
            ffn_kernel((), (), streams)
        else:
            mix_kernel(jobs[stage // 2], ids, streams)
        Step.now = None
        if s == 3:
            for k in range(10 * stage, 10 * stage + 10):
                finished.append(move(values[k], results[k]))

    tasks = {FIRST_TASK[stage] + s: (stage, s) for stage in range(3) for s in range(4)}
    from_x, from_y, low, high = [], [], [], []
    for step in range(max(len(segments) + 2, max(tasks) + 1)):
        if step < len(segments):
            segment = segments[step]
            for item in arrivals[step]:
                item.wait_recv()
            from_x.append(pass_on(segment, 0, across))
            from_y.append(pass_on(segment, 0, along))
            late[stage_of[segment[0]]].append(pass_on(segment, 0, core))
        if 0 <= step - 1 < len(segments):
            segment = segments[step - 1]
            from_x[step - 1].wait_recv()
            low.append(pass_on(segment, 2, along, 0, 0))
            from_y[step - 1].wait_recv()
            high.append(pass_on(segment, 4, across, 1, 1))
            late[stage_of[segment[0]]].append(pass_on(segment, 2, core))
            late[stage_of[segment[0]]].append(pass_on(segment, 4, core))
        if 0 <= step - 2 < len(segments):
            segment = segments[step - 2]
            low[step - 2].wait_recv()
            high[step - 2].wait_recv()
            late[stage_of[segment[0]]].append(pass_on(segment, 6, core))
        if step in tasks:
            run(*tasks[step])
    for item in late[3]:
        item.wait_recv()
    for item in copies:
        item.wait_send()
    for item in finished:
        item.wait()


def gather(stages, row, states, rows, ids, jobs, places):
    mats = [item for stage in stages for item in stage]
    stage_of = [k for k, stage in enumerate(stages) for _ in stage]
    segments = segments_of(mats)
    inputs = [local for local, _ in mats] + [row]
    weights = [jax.ShapeDtypeStruct((4,) + local.shape, bf16) for local, _ in mats]
    weights.append(jax.ShapeDtypeStruct((3,) + row.shape, bf16))
    shapes = early_outs(jobs, [count for _, count in places], states)
    results = [jax.ShapeDtypeStruct(shape, dtype) for shape, dtype in shapes]
    anywhere, near = pl.BlockSpec(memory_space=pl.ANY), pl.BlockSpec(memory_space=pltpu.VMEM)
    total = 12 * len(segments) + len(mats) + 3
    tops = [
        (max(inputs[EARLY[stage][k][part]].shape[0] for stage in range(3)), states[k].shape[1])
        for k in range(2)
        for part in range(2)
    ]
    found = pl.pallas_call(
        functools.partial(gather_kernel, segments, stage_of, len(mats), jobs, places, shapes),
        out_shape=weights + results,
        in_specs=[anywhere] * len(inputs) + [near] * 12,
        out_specs=[anywhere] * (len(weights) + len(results)),
        scratch_shapes=[pltpu.VMEM(shape, dtype) for shape, dtype in shapes]
        + [pltpu.VMEM((2,) + top, bf16) for top in tops]
        + [pltpu.VMEM((4,) + row.shape, bf16)]
        + [pltpu.SemaphoreType.DMA((total,))] * 2
        + [pltpu.SemaphoreType.DMA((48 + 30 + 2,))],
        compiler_params=pltpu.CompilerParams(collective_id=0, has_side_effects=True),
        name="gather",
    )(*inputs, *states, *rows, *ids)
    whole = [out.reshape(-1, out.shape[2]) for out in found[: len(mats)]]
    values = found[len(weights) :]
    return whole, found[len(mats)], [values[5 * k : 5 * k + 5] for k in range(6)]


def gather_plain(stages, row):
    tensor = lax.axis_size("tensor")
    whole = [
        jnp.concatenate([local] + [swap(local, "tensor", s) for s in range(1, tensor)])
        for stage in stages
        for local, _ in stage
    ]
    return whole, jnp.stack([swap(row, "tensor", s) for s in range(1, tensor)])


def wide(value):
    return value.astype(f32)


def reduce_plain(chunks, lefts, rights):
    tensor = lax.axis_size("tensor")
    done = []
    for _, terms in chunks:
        blocks = []
        for s in range(tensor):
            total = 0
            for left, right, column in terms:
                first = s * (rights[right].shape[1] // tensor) + column
                total = total + outer_sum(
                    lefts[left].astype(bf16), rights[right][:, first : first + LANES]
                )
            blocks.append(total)
        mine = lax.psum_scatter(
            jnp.stack(blocks, axis=1).astype(bf16), "dp", scatter_dimension=0, tiled=True
        )
        summed = wide(mine[:, 0])
        for s in range(1, tensor):
            summed = summed + wide(swap(mine[:, s], "tensor", s))
        done.append(summed)
    return jnp.concatenate(done)


TILE = 32
RING = 6


def backward_kernel(stages, counts, places, n_weights, *refs):
    n = len(stages)
    weights, refs = refs[:n_weights], refs[n_weights:]
    saved, refs = refs[: 10 * n], refs[10 * n :]
    uppers_in, rows, ids, refs = refs[:2], refs[2 : 2 + 2 * n], refs[2 + 2 * n : 6 + 2 * n], refs[6 + 2 * n :]
    final, refs = refs[:n], refs[n:]
    deltas, bias_out, sums_out, refs = refs[:2], refs[2], refs[3:5], refs[5:]
    landed, refs = refs[: 4 * n], refs[4 * n :]
    core_in, square_in, turn_in, line_in = (landed[k * n : (k + 1) * n] for k in range(4))
    reduce_scratch, refs = refs[:11], refs[11:]
    (
        own_buffer,
        core_out,
        core_buffer,
        kept,
        square_out,
        square_buffer,
        turn_out,
        turn_buffer,
        line_out,
        line_buffer,
        sums,
    ) = reduce_scratch
    small, small_in, bias_in, refs = refs[:3], refs[3:6], refs[6], refs[7:]
    blocks, refs = refs[:4], refs[4:]
    hidden_block, mixed_block, refs = refs[:2], refs[2:4], refs[4:]
    normed, scales, upstream, branch, refs = refs[:2], refs[2:4], refs[4:6], refs[6:8], refs[8:]
    states, first_right, second_right, refs = refs[:2], refs[2:4], refs[4:6], refs[6:]
    picked, turned, upper_block, refs = refs[:4], refs[4:6], refs[6:10], refs[10:]
    send_sems, recv_sems, local_sems = refs
    me, place_t = lax.axis_index("dp"), lax.axis_index("tensor")
    lines = [{"tensor": jnp.bitwise_xor(place_t, s)} for s in range(1, 4)]
    core, across, along = [{"dp": jnp.bitwise_xor(me, mask)} for mask in (1, 2, 4)]
    greet(lines + [core, across, along])
    remote, local = [], []

    def send(source, target, device):
        k = len(remote)
        item = pltpu.make_async_remote_copy(
            source, target, send_sems.at[k], recv_sems.at[k], device_id=device, device_id_type=MESH
        )
        item.start()
        remote.append(item)
        return item

    def move(source, target):
        item = pltpu.make_async_copy(source, target, local_sems.at[len(local)])
        item.start()
        local.append(item)
        return item

    def each_tile(count, body):
        def step(index, carry):
            body(pl.ds(pl.multiple_of(index * TILE, TILE), TILE))
            return carry

        lax.fori_loop(0, count // TILE, step, 0)

    pairs = [(stage, i) for stage in range(n) for i in range(2)]
    core_sends, square_sends, turn_sends, line_sends = {}, {}, {}, {}

    def saved_of(stage, k):
        return saved[(2 * stage + k) * 5 : (2 * stage + k + 1) * 5]

    start_loads, block_loads, slope_loads = {}, {}, {}

    def block_ref(stage, k):
        wide_kind = stages[stage][0] == "ffn"
        ref = (hidden_block if wide_kind else mixed_block)[k]
        return ref, saved_of(stage, k)[0].shape[1] // 4

    def load_block(stage, s):
        items = []
        for k in range(2):
            first, second = stages[stage][2][k]
            for part, index in ((0, first), (1, second)):
                if part and first == second:
                    continue
                source = weights[index]
                items.append(move(source.at[s], blocks[2 * k + part].at[pl.ds(0, source.shape[1])]))
            ref, width = block_ref(stage, k)
            source = saved_of(stage, k)[0]
            items.append(move(source.at[:, pl.ds(s * width, width)], ref.at[:, pl.ds(0, width)]))
        block_loads[stage, s] = items

    def load_start(stage):
        items = []
        for k in range(2):
            items.append(move(saved_of(stage, k)[1], normed[k]))
            items.append(move(saved_of(stage, k)[2], scales[k]))
        start_loads[stage] = items
        load_block(stage, 0)

    def load_slopes(stage):
        items = []
        for k in range(2):
            source = saved_of(stage, k)[3]
            items.append(move(source, second_right[k].at[:, pl.ds(0, source.shape[1])]))
            items.append(move(saved_of(stage, k)[4], states[k]))
        slope_loads[stage] = items

    def back(stage, s):
        kind, jobs, indices, norm, _ = stages[stage]
        if s == 0:
            for item in start_loads[stage]:
                item.wait()
        for item in block_loads[stage, s]:
            item.wait()
        streams = []
        for k in range(2):
            first, second = indices[k]
            weight = blocks[2 * k].at[pl.ds(0, weights[first].shape[1])]
            other = blocks[2 * k + 1].at[pl.ds(0, weights[second].shape[1])]
            if first == second:
                other = weight
            ref, width = block_ref(stage, k)
            at, count = places[2 * norm + k]
            ins = (upstream[k], normed[k], scales[k], rows[2 * stage + k], ref.at[:, pl.ds(0, width)])
            outs = [
                upstream[k],
                branch[k],
                small[1 + k].at[norm],
                first_right[k].at[:, pl.ds(s * width, width)],
                small[0].at[s, :, pl.ds(at, count)],
            ]
            if kind == "mix":
                size, heads = jobs[k][2], jobs[k][3]
                outs.append(upper_block[2 * (stage // 2) + k])
            streams.append(((*ins, weight, other), outs))
        Step.now = s
        if kind == "ffn":
            ffn_back_kernel((), (), streams)
        else:
            mix_back_kernel(jobs, ids, streams)
        Step.now = None
        if s < 3:
            load_block(stage, s + 1)
        elif stage + 1 < n:
            load_start(stage + 1)

    def produce(pair):
        stage, i = pairs[pair]
        if i == 0:
            for item in slope_loads[stage]:
                item.wait()
            for index, left in enumerate((states[0], branch[0], states[1], branch[1])):
                whole, target = turned[index // 2], picked[index]
                count = target.shape[0] // 8
                whole[...] = wide(left[...]).T.astype(bf16)
                for q in range(8):
                    owner = jnp.bitwise_xor(me, 2 * (q % 4) + q // 4)
                    first = pl.multiple_of(owner * count, 32)
                    target[q * count : (q + 1) * count, :] = whole[pl.ds(first, count), :]
        rights = (first_right[0], second_right[0], first_right[1], second_right[1])
        for half in range(2):
            slot, at = (2 * pair + half) % 4, 0
            if pair >= 2:
                core_sends[pair - 2, half].wait_send()
            for count, repeat, terms in stages[stage][4]:

                def chunk(index, carry):
                    total = None
                    for left, width, column in terms:
                        base = (2 * half + i) * width + column
                        part = pl.ds(pl.multiple_of(base + index * LANES, LANES), LANES)
                        term = jnp.dot(
                            picked[left][...], rights[left][:, part], preferred_element_type=f32
                        )
                        total = term if total is None else total + term
                    to = pl.ds(pl.multiple_of(at + index * count, 32), count)
                    for q in range(8):
                        minor = q % 4
                        place_q = 2 * (minor % 2) + minor // 2 if half == 0 else minor
                        target = core_out if q >= 4 else own_buffer
                        target[slot, place_q, to, :] = total[q * count : (q + 1) * count, :].astype(bf16)
                    return carry

                if repeat == 1:
                    chunk(0, 0)
                else:
                    lax.fori_loop(0, repeat, chunk, 0)
                at += count * repeat
            core_sends[pair, half] = send(
                core_out.at[slot, :, pl.ds(0, counts[stage])], core_in[stage].at[half, :, i], core
            )

    def slot_of(pair, half):
        return (2 * pair + half) % RING

    def square(pair):
        stage, i = pairs[pair]
        count, loads = counts[stage], []
        for half in range(2):
            core_sends[pair, half].wait_recv()
            loads.append(
                move(core_in[stage].at[half, :, i], core_buffer.at[half, :, pl.ds(0, count)])
            )
        for half in range(2):
            loads[half].wait()
            at, buffer = slot_of(pair, half), (2 * pair + half) % 4

            def body(tile):
                for q in range(4):
                    value = wide(own_buffer[buffer, q, tile, :]) + wide(core_buffer[half, q, tile, :])
                    target = kept if q < 2 else square_out
                    target[at, q % 2, tile, :] = value.astype(bf16)

            if pair >= RING // 2:
                square_sends[pair - RING // 2, half].wait_send()
            each_tile(count, body)
            square_sends[pair, half] = send(
                square_out.at[at, :, pl.ds(0, count)],
                square_in[stage].at[half, i],
                along if half else across,
            )

    def turn(pair):
        stage, i = pairs[pair]
        count, loads = counts[stage], []
        for half in range(2):
            square_sends[pair, half].wait_recv()
            loads.append(move(square_in[stage].at[half, i], square_buffer.at[half, :, pl.ds(0, count)]))
        for half in range(2):
            loads[half].wait()
            at = slot_of(pair, half)

            def body(tile):
                first = wide(kept[at, 0, tile, :]) + wide(square_buffer[half, 0, tile, :])
                kept[at, 0, tile, :] = first.astype(bf16)
                second = wide(kept[at, 1, tile, :]) + wide(square_buffer[half, 1, tile, :])
                turn_out[at, tile, :] = second.astype(bf16)

            if pair >= RING // 2:
                turn_sends[pair - RING // 2, half].wait_send()
            each_tile(count, body)
            turn_sends[pair, half] = send(
                turn_out.at[at, pl.ds(0, count)],
                turn_in[stage].at[half, i],
                across if half else along,
            )

    results = {}

    def line(pair):
        stage, i = pairs[pair]
        count, loads = counts[stage], []
        for half in range(2):
            turn_sends[pair, half].wait_recv()
            loads.append(move(turn_in[stage].at[half, i], turn_buffer.at[half, pl.ds(0, count)]))
        if i == 0 and stage >= 2:
            results[stage - 2].wait()
        for half in range(2):
            loads[half].wait()
            at, s = slot_of(pair, half), 2 * half + i

            def body(tile):
                value = wide(kept[at, 0, tile, :]) + wide(turn_buffer[half, tile, :])
                if s == 0:
                    sums[stage % 2, tile, :] = value
                else:
                    line_out[at, tile, :] = value.astype(bf16)

            if s and at in line_last:
                line_last.pop(at).wait_send()
            each_tile(count, body)
            if s:
                line_sends[pair, half] = send(
                    line_out.at[at, pl.ds(0, count)], line_in[stage].at[s - 1], lines[s - 1]
                )
                line_last[at] = line_sends[pair, half]

    line_last = {}

    def finish_stage(stage):
        count = counts[stage]
        for pair, half in ((2 * stage, 1), (2 * stage + 1, 0), (2 * stage + 1, 1)):
            line_sends[pair, half].wait_recv()
        move(line_in[stage], line_buffer.at[:, pl.ds(0, count)]).wait()

        def body(tile):
            value = sums[stage % 2, tile, :] + wide(line_buffer[0, tile, :])
            sums[stage % 2, tile, :] = (
                value + wide(line_buffer[1, tile, :]) + wide(line_buffer[2, tile, :])
            )

        each_tile(count, body)
        results[stage] = move(sums.at[stage % 2, pl.ds(0, count)], final[stage])

    small_sends, bias_sends = [], []
    steps = [core, across, along, lines[0], lines[1]]

    def small_step(k):
        if k:
            for index, item in enumerate(small_sends[k - 1]):
                item.wait_recv()
                item.wait_send()
                if item is not None:
                    arr = 3 - len(small_sends[k - 1]) + index
                    small[arr][...] = small[arr][...] + small_in[arr][k - 1]
        if k < 5:
            chosen = (0, 1, 2) if k < 3 else (1, 2)
            small_sends.append([send(small[arr], small_in[arr].at[k], steps[k]) for arr in chosen])
        if k == 3:
            for s in range(1, 4):
                bias_sends.append(send(small[0].at[s], bias_in.at[s - 1], lines[s - 1]))

    first_loads = [move(uppers_in[k], upstream[k]) for k in range(2)]
    load_start(0)
    load_slopes(0)
    for item in first_loads:
        item.wait()
    for s in range(4):
        back(0, s)
    produce(0)
    delta_moves = []
    for step in range(len(pairs) + 3):
        following = step // 2 + 1 if step % 2 == 0 and step // 2 + 1 < n else None
        if step < len(pairs):
            square(step)
            if step + 1 < len(pairs):
                produce(step + 1)
        if following is not None:
            load_slopes(following)
            back(following, 0)
            back(following, 1)
        if 0 <= step - 1 < len(pairs):
            turn(step - 1)
        if following is not None:
            back(following, 2)
        if 0 <= step - 2 < len(pairs):
            line(step - 2)
        if following is not None:
            back(following, 3)
        if following == n - 1:
            delta_moves += [move(upstream[k], deltas[k]) for k in range(2)]
        if step >= 3 and (step - 3) % 2:
            finish_stage((step - 3) // 2)
        if 0 <= step - 5 <= 5:
            small_step(step - 5)
    for item in bias_sends:
        item.wait_recv()
        item.wait_send()
    total = small[0][0]
    for k in range(3):
        total = total + bias_in[k]
    small[0][0] = total
    delta_moves.append(move(small[0].at[0], bias_out))
    delta_moves += [move(small[1 + k], sums_out[k]) for k in range(2)]
    for item in delta_moves + [results[n - 2], results[n - 1]]:
        item.wait()
    for group, lag in ((core_sends, 2), (square_sends, RING // 2), (turn_sends, RING // 2)):
        for (pair, half), item in group.items():
            if pair + lag >= len(pairs):
                item.wait_send()
    for item in line_last.values():
        item.wait_send()


def backward_all(stages, counts, places, weights, saved, uppers, rows, ids):
    n, top = len(stages), max(counts)
    anywhere, near = pl.BlockSpec(memory_space=pl.ANY), pl.BlockSpec(memory_space=pltpu.VMEM)
    landed = (
        [jax.ShapeDtypeStruct((2, 4, 2, count, LANES), bf16) for count in counts]
        + [jax.ShapeDtypeStruct((2, 2, 2, count, LANES), bf16) for count in counts]
        + [jax.ShapeDtypeStruct((2, 2, count, LANES), bf16) for count in counts]
        + [jax.ShapeDtypeStruct((3, count, LANES), bf16) for count in counts]
    )
    shapes = [item.shape for item in uppers]
    columns = sum(count for _, count in places)
    outs = [jax.ShapeDtypeStruct((count, LANES), f32) for count in counts]
    outs += [jax.ShapeDtypeStruct(shape, f32) for shape in shapes]
    outs.append(jax.ShapeDtypeStruct((1, columns), f32))
    outs += [jax.ShapeDtypeStruct((4, 3, shape[1]), f32) for shape in shapes]
    kinds = [stage[0] for stage in stages]

    def widest(position, k, kind=None):
        return max(
            saved[(2 * stage + k) * 5 + position].shape[1]
            for stage in range(n)
            if kind in (None, kinds[stage])
        )

    smalls = [(4, 1, columns)] + [(4, 3, shape[1]) for shape in shapes]
    scratch = [
        pltpu.VMEM((4, 4, top, LANES), bf16),
        pltpu.VMEM((4, 4, top, LANES), bf16),
        pltpu.VMEM((2, 4, top, LANES), bf16),
        pltpu.VMEM((RING, 2, top, LANES), bf16),
        pltpu.VMEM((RING, 2, top, LANES), bf16),
        pltpu.VMEM((2, 2, top, LANES), bf16),
        pltpu.VMEM((RING, top, LANES), bf16),
        pltpu.VMEM((2, top, LANES), bf16),
        pltpu.VMEM((RING, top, LANES), bf16),
        pltpu.VMEM((3, top, LANES), bf16),
        pltpu.VMEM((2, top, LANES), f32),
    ]
    scratch += [pltpu.VMEM(shape, f32) for shape in smalls]
    scratch += [pltpu.VMEM((5 if k else 3,) + shape, f32) for k, shape in enumerate(smalls)]
    scratch.append(pltpu.VMEM((3, 1, columns), f32))
    for k in range(2):
        for part in range(2):
            rows_max = max(
                weights[stage[2][k][part]].shape[1]
                for stage in stages
                if not (part and stage[2][k][0] == stage[2][k][1])
            )
            scratch.append(pltpu.VMEM((rows_max, shapes[k][1]), bf16))
    scratch += [pltpu.VMEM((shapes[k][0], widest(0, k, "ffn") // 4), f32) for k in range(2)]
    scratch += [pltpu.VMEM((shapes[k][0], widest(0, k, "mix") // 4), bf16) for k in range(2)]
    scratch += [pltpu.VMEM(shape, f32) for shape in shapes]
    scratch += [pltpu.VMEM((shape[0], 128), f32) for shape in shapes]
    scratch += [pltpu.VMEM(shape, f32) for shape in shapes]
    scratch += [pltpu.VMEM(shape, bf16) for shape in shapes]
    scratch += [pltpu.VMEM(shape, f32) for shape in shapes]
    scratch += [pltpu.VMEM((shapes[k][0], widest(0, k)), bf16) for k in range(2)]
    scratch += [pltpu.VMEM((shapes[k][0], widest(3, k)), bf16) for k in range(2)]
    scratch += [pltpu.VMEM(shapes[k // 2][::-1], bf16) for k in range(4)]
    scratch += [pltpu.VMEM(shape[::-1], bf16) for shape in shapes]
    for stage in (1, 3):
        for k in range(2):
            scratch.append(pltpu.VMEM((shapes[k][0], stages[stage][1][k][2] * stages[stage][1][k][3]), bf16))
    remote = 15 * n + 16
    scratch += [pltpu.SemaphoreType.DMA((remote,))] * 2 + [pltpu.SemaphoreType.DMA((64 * n,))]
    found = pl.pallas_call(
        functools.partial(backward_kernel, stages, counts, places, len(weights)),
        out_shape=outs + landed,
        in_specs=[anywhere] * (len(weights) + len(saved) + 2) + [near] * (2 * n + 4),
        out_specs=[anywhere] * (len(outs) + len(landed)),
        scratch_shapes=scratch,
        compiler_params=pltpu.CompilerParams(
            collective_id=1, has_side_effects=True, vmem_limit_bytes=67000000
        ),
        name="backward",
    )(*weights, *saved, *uppers, *rows, *ids)
    return found[:n], found[n : n + 2], found[n + 2], found[n + 3 : n + 5]


def split_packed(packed, layout):
    found, at = [], 0
    for rows, count, parts in layout:
        whole = jnp.concatenate(
            [packed[at + k * rows : at + (k + 1) * rows] for k in range(count)], axis=1
        )
        at += rows * count
        first = 0
        for kind, columns in parts:
            part = whole[:, first : first + columns]
            first += columns
            if kind == "cube":
                part = part.reshape(rows, 3, columns // 3)
            found.append(part.T if kind == "turn" else part)
    return found


def unpack_kernel(layouts, *refs):
    n = len(layouts)
    n_out = sum(len(parts) for layout in layouts for _, _, parts in layout)
    packed, outs, line = refs[:n], refs[n : n + n_out], refs[n + n_out]
    index = 0
    for source, layout in zip(packed, layouts):
        at = 0
        for rows, count, parts in layout:
            for k in range(count):
                line[:rows, k * LANES : (k + 1) * LANES] = source[at + k * rows : at + (k + 1) * rows, :]
            at += rows * count
            first = 0
            for kind, columns in parts:
                out = outs[index]
                if kind == "flat":
                    out[...] = line[:rows, first : first + columns]
                elif kind == "turn":
                    block = line[:rows, first : first + columns]
                    out[...] = block.T if rows % 128 == 0 else block
                else:
                    for k in range(3):
                        start = first + k * (columns // 3)
                        out[k, :, :] = line[:rows, start : start + columns // 3]
                index += 1
                first += columns


def unpack(packed, layouts):
    if lax.axis_size("dp") != 8:
        return [item for value, layout in zip(packed, layouts) for item in split_packed(value, layout)]
    shapes, top, widest = [], 0, 0
    for layout in layouts:
        for rows, count, parts in layout:
            top, widest = max(top, rows), max(widest, count * LANES)
            for kind, columns in parts:
                shapes.append(
                    {
                        "flat": (rows, columns),
                        "turn": (columns, rows) if rows % 128 == 0 else (rows, columns),
                        "cube": (3, rows, columns // 3),
                    }[kind]
                )
    found = pl.pallas_call(
        functools.partial(unpack_kernel, layouts),
        out_shape=[jax.ShapeDtypeStruct(shape, f32) for shape in shapes],
        scratch_shapes=[pltpu.VMEM((top, widest), f32)],
        name="unpack",
    )(*packed)
    kinds = [(kind, rows) for layout in layouts for rows, _, parts in layout for kind, _ in parts]
    return [
        item.transpose(1, 0, 2)
        if kind == "cube"
        else (item.T if kind == "turn" and rows % 128 else item)
        for item, (kind, rows) in zip(found, kinds)
    ]


def row_sum(value):
    return jnp.sum(wide(value), axis=0, keepdims=True)


class Step:
    now = None


def on_first(body):
    if Step.now is None:
        pl.when(pl.program_id(0) == 0)(body)
    elif Step.now == 0:
        body()


def on_later(body):
    if Step.now is None:
        pl.when(pl.program_id(0) > 0)(body)
    elif Step.now > 0:
        body()


def on_last(body):
    if Step.now is None:
        pl.when(pl.program_id(0) == pl.num_programs(0) - 1)(body)
    elif Step.now == 3:
        body()


def attend_probs(query, key, allowed, scale):
    scores = times_transpose(query, key) * scale
    scores = jnp.where(allowed, scores, -1e30)
    weights = jnp.exp(scores - jnp.max(scores, axis=1, keepdims=True))
    return weights / jnp.sum(weights, axis=1, keepdims=True)


def attend(jobs, mixed, ids, outs):
    for asks, gives, size, heads, shift in jobs:
        width = size * heads
        allowed = ids[2 * asks][...] == ids[2 * gives + 1][...]
        if shift:
            outs[asks][:, :shift] = jnp.zeros((outs[asks].shape[0], shift), bf16)
        for head in range(heads):
            at = head * size
            probs = attend_probs(
                mixed[asks][:, at : at + size],
                mixed[gives][:, width + at : width + at + size],
                allowed,
                1.0 / math.sqrt(size),
            )
            context = times(
                probs.astype(bf16), mixed[gives][:, 2 * width + at : 2 * width + at + size]
            )
            outs[asks][:, shift + at : shift + at + size] = context.astype(bf16)


def attend_back(jobs, mixed, ids, uppers, outs):
    for asks, gives, size, heads, shift in jobs:
        width = size * heads
        scale = 1.0 / math.sqrt(size)
        allowed = ids[2 * asks][...] == ids[2 * gives + 1][...]
        if shift:
            outs[asks][:, shift:] = jnp.zeros((outs[asks].shape[0], width), bf16)
        for head in range(heads):
            at = head * size
            query = mixed[asks][:, at : at + size]
            key = mixed[gives][:, width + at : width + at + size]
            value = mixed[gives][:, 2 * width + at : 2 * width + at + size]
            upper = uppers[asks][:, at : at + size]
            probs = attend_probs(query, key, allowed, scale)
            prob_delta = times_transpose(upper, value)
            inner = jnp.sum(prob_delta * probs, axis=1, keepdims=True)
            score_delta = (probs * (prob_delta - inner)).astype(bf16)
            outs[asks][:, at : at + size] = (times(score_delta, key) * scale).astype(bf16)
            outs[gives][:, width + at : width + at + size] = (
                outer_sum(score_delta, query) * scale
            ).astype(bf16)
            outs[gives][:, 2 * width + at : 2 * width + at + size] = outer_sum(
                probs.astype(bf16), upper
            ).astype(bf16)


def finish(state, total, rows, outs):
    branch = total[...] + rows[0:1, :]
    outs[0][...], outs[1][...], scale = norm_forward(
        wide(state[...]) + branch, rows[1:2, :], rows[2:3, :]
    )
    outs[2][...] = jnp.broadcast_to(scale, outs[2].shape)


def add_to(target, value):
    @on_first
    def _():
        target[...] = value

    @on_later
    def _():
        target[...] += value


def begin_back(upstream, saved, rows, outs):
    @on_first
    def _():
        upper, normed = upstream[...], saved[0][...]
        hidden_delta = norm_backward(upper, normed, saved[1][:, 0:1], rows[1:2, :])
        branch_delta = hidden_delta.astype(bf16)
        outs[0][...] = hidden_delta
        outs[1][...] = branch_delta
        outs[2][0:1, :] = row_sum(branch_delta)
        outs[2][1:2, :] = row_sum(upper * normed)
        outs[2][2:3, :] = row_sum(upper)


def mix_kernel(jobs, ids, streams):
    for (state, weight, output, offset, rows), (mixed, context, *final) in streams:
        mixed[...] = (times_transpose(state[...].astype(bf16), weight[...]) + wide(offset[...])).astype(bf16)
    attend(jobs, [out[0] for _, out in streams], ids, [out[1] for _, out in streams])
    for (asks, _, _, _, shift), (ins, outs) in zip(jobs, streams):
        state, output, rows = ins[0], ins[2], ins[4]
        add_to(outs[2], times(outs[1][:, shift:], output[shift:, :]))

        @on_last
        def _():
            finish(state, outs[2], rows, outs[2:])


def mix_back_kernel(jobs, ids, streams):
    for (asks, _, size, heads, shift), (ins, outs) in zip(jobs, streams):
        upstream, normed, scale, rows, mixed, weight, output = ins
        input_delta, branch_delta, sums, flat, bias, upper = outs
        begin_back(upstream, (normed, scale), rows, (input_delta, branch_delta, sums))
        upper[...] = times_transpose(branch_delta[...], output[shift:, :]).astype(bf16)
    attend_back(
        jobs,
        [ins[4] for ins, _ in streams],
        ids,
        [outs[5] for _, outs in streams],
        [outs[3] for _, outs in streams],
    )
    for (_, _, _, _, shift), (ins, outs) in zip(jobs, streams):
        width = shift or outs[3].shape[1]
        outs[4][...] = row_sum(outs[3][...])
        outs[0][...] += times(outs[3][:, :width], ins[5][:width, :])


def ffn_kernel(jobs, ids, streams):
    for (state, expand, reduce_weight, offset, rows), outs in streams:
        hidden, active, *final = outs
        value = times_transpose(state[...].astype(bf16), expand[...]) + wide(offset[...])
        hidden[...] = value
        active[...] = gelu_value(value).astype(bf16)
        add_to(final[0], times(active[...], reduce_weight[...]))

        @on_last
        def _():
            finish(state, final[0], rows, final)


def ffn_back_kernel(jobs, ids, streams):
    for ins, outs in streams:
        upstream, normed, scale, rows, hidden, expand, reduce_weight = ins
        input_delta, branch_delta, sums, inner, bias = outs
        begin_back(upstream, (normed, scale), rows, (input_delta, branch_delta, sums))
        active_delta = times_transpose(branch_delta[...], reduce_weight[...])
        inner[...] = (active_delta * gelu_slope(hidden[...])).astype(bf16)
        bias[...] = row_sum(inner[...])
        input_delta[...] += times(inner[...], expand[...])


def stage_kernel(body, jobs, n_ids, n_ins, n_outs, n_scratch, *refs):
    ids, at, streams = refs[:n_ids], n_ids, []
    n = len(refs[n_ids:]) // 2
    total_in, total_out = 2 * n_ins, 2 * n_outs
    ins = refs[n_ids : n_ids + total_in]
    outs = refs[n_ids + total_in : n_ids + total_in + total_out]
    scratch = refs[n_ids + total_in + total_out :]
    for k in range(2):
        streams.append(
            (
                ins[k * n_ins : (k + 1) * n_ins],
                [
                    *outs[k * n_outs : (k + 1) * n_outs],
                    *scratch[k * n_scratch : (k + 1) * n_scratch],
                ],
            )
        )
    body(jobs, ids, streams)


def run_stage(body, name, jobs, ids, streams, scratch=((), ())):
    steps = lax.axis_size("tensor")

    def spec(shape, how):
        if how is None:
            return pl.BlockSpec(shape, lambda s: (0, 0))
        block = tuple(size // steps if k == how else size for k, size in enumerate(shape))
        return pl.BlockSpec(block, (lambda s: (s, 0)) if how == 0 else (lambda s: (0, s)))

    ins = [item for stream in streams for item in stream[0]]
    outs = [item for stream in streams for item in stream[1]]
    found = pl.pallas_call(
        functools.partial(
            stage_kernel, body, jobs, len(ids), len(streams[0][0]), len(streams[0][1]), len(scratch[0])
        ),
        grid=(steps,),
        out_shape=[jax.ShapeDtypeStruct(shape, dtype) for shape, dtype, _ in outs],
        in_specs=[spec(item.shape, None) for item in ids]
        + [spec(item.shape, how) for item, how in ins],
        out_specs=[spec(shape, how) for shape, _, how in outs],
        scratch_shapes=[pltpu.VMEM(shape, bf16) for group in scratch for shape in group],
        cost_estimate=pl.CostEstimate(flops=0, bytes_accessed=0, transcendentals=0),
        name=name,
    )(*ids, *[item for item, _ in ins])
    half = len(streams[0][1])
    return found[:half], found[half:]


def final_shapes(state):
    return [(state.shape, f32, None), (state.shape, f32, None), ((state.shape[0], 128), f32, None)]


def mix_forward(name, jobs, ids, streams):
    tensor, groups = lax.axis_size("tensor"), []
    for (_, _, size, heads, shift), (state, weight, output, offset, rows) in zip(jobs, streams):
        ins = [(state, None), (weight, 0), (output, 0), (offset, 1), (rows, None)]
        tokens = state.shape[0]
        outs = [
            ((tokens, weight.shape[0]), bf16, 1),
            ((tokens, (shift + size * heads) * tensor), bf16, 1),
        ] + final_shapes(state)
        groups.append((ins, outs))
    return run_stage(mix_kernel, name, jobs, ids, groups)


def back_shapes(upstream, columns):
    tokens, width = upstream.shape
    return [
        (upstream.shape, f32, None),
        (upstream.shape, bf16, None),
        ((3, width), f32, None),
        ((tokens, columns), bf16, 1),
        ((1, columns), f32, 1),
    ]


def mix_backward(name, jobs, ids, streams):
    groups, scratch = [], []
    for (_, _, size, heads, _), (upstream, kept, weight, output, rows) in zip(jobs, streams):
        mixed, _, _, normed, scale = kept
        ins = [(upstream, None), (normed, None), (scale, None), (rows, None)]
        ins += [(mixed, 1), (weight, 0), (output, 0)]
        groups.append((ins, back_shapes(upstream, mixed.shape[1])))
        scratch.append([(upstream.shape[0], size * heads)])
    return run_stage(mix_back_kernel, name, jobs, ids, groups, scratch)


def ffn_forward(name, streams):
    groups = []
    for state, expand, reduce_weight, offset, rows in streams:
        ins = [(state, None), (expand, 0), (reduce_weight, 0), (offset, 1), (rows, None)]
        shape = (state.shape[0], expand.shape[0])
        groups.append((ins, [(shape, f32, 1), (shape, bf16, 1)] + final_shapes(state)))
    return run_stage(ffn_kernel, name, (), (), groups)


def ffn_backward(name, streams):
    groups = []
    for upstream, kept, expand, reduce_weight, rows in streams:
        hidden, _, _, normed, scale = kept
        ins = [(upstream, None), (normed, None), (scale, None), (rows, None)]
        ins += [(hidden, 1), (expand, 0), (reduce_weight, 0)]
        groups.append((ins, back_shapes(upstream, hidden.shape[1])))
    return run_stage(ffn_back_kernel, name, (), (), groups)


def bias_parts(sums, width):
    summed = sums.reshape(lax.axis_size("tensor"), -1)
    return jnp.stack([summed[:, :width], summed[:, 2 * width : 3 * width]], axis=1)


def plain_chunks(rows, left, width):
    return [(rows, [(left, left, at)]) for at in range(0, width, LANES)]


def per_device(
    text,
    image,
    text_segment,
    image_segment,
    text_cross_weight,
    text_cross_bias,
    text_cross_output,
    text_inner_expand,
    text_inner_offset,
    text_inner_reduce,
    text_self_weight,
    text_self_bias,
    text_self_output,
    text_outer_expand,
    text_outer_offset,
    text_outer_reduce,
    text_branch_bias,
    text_norm_gain,
    text_norm_shift,
    image_cross_weight,
    image_cross_bias,
    image_cross_output,
    image_inner_expand,
    image_inner_offset,
    image_inner_reduce,
    image_self_weight,
    image_self_bias,
    image_self_output,
    image_outer_expand,
    image_outer_offset,
    image_outer_reduce,
    image_branch_bias,
    image_norm_gain,
    image_norm_shift,
    text_cotangent,
    image_cotangent,
):
    tensor = lax.axis_size("tensor")
    place_t = lax.axis_index("tensor")
    dp = lax.axis_size("dp")
    count = text_segment.shape[0] // tensor
    captions = 4
    row_id = captions * jnp.arange(count, dtype=jnp.int32)[:, None]
    text_id = lax.dynamic_slice_in_dim(text_segment, place_t * count, count, 0) + row_id
    image_id = lax.dynamic_slice_in_dim(image_segment, place_t * count, count, 0) + row_id
    ids = [
        text_id.reshape(-1, 1),
        text_id.reshape(1, -1),
        image_id.reshape(-1, 1),
        image_id.reshape(1, -1),
    ]
    text_gain, text_shift = wide(text_norm_gain), wide(text_norm_shift)
    image_gain, image_shift = wide(image_norm_gain), wide(image_norm_shift)

    bias_order = (
        text_cross_bias,
        image_cross_bias,
        text_inner_offset,
        image_inner_offset,
        text_self_bias,
        image_self_bias,
        text_outer_offset,
        image_outer_offset,
    )
    def spread(bias, blank):
        zero = jnp.zeros_like(bias[0])
        return [bias[0], zero, bias[1]] + ([zero] if blank else [])

    bias_row = jnp.concatenate(
        [
            *spread(text_cross_bias, False),
            *spread(image_cross_bias, False),
            text_inner_offset,
            image_inner_offset,
            *spread(text_self_bias, True),
            *spread(image_self_bias, False),
            text_outer_offset,
            image_outer_offset,
        ]
    ).reshape(1, -1)
    places = early_columns(
        3 * text_cross_bias.shape[1],
        3 * image_cross_bias.shape[1],
        text_inner_offset.shape[0],
        image_inner_offset.shape[0],
        4 * text_self_bias.shape[1],
        3 * image_self_bias.shape[1],
    )

    def turned(weight):
        return weight.reshape(weight.shape[0], -1).T

    def single(*locals_):
        return [(local, [local.shape[0]]) for local in locals_]

    text_qkv = turned(text_self_weight)
    text_both = jnp.concatenate([text_qkv, text_self_output], axis=0)
    stages = [
        single(turned(text_cross_weight), text_cross_output, turned(image_cross_weight), image_cross_output),
        single(turned(text_inner_expand), text_inner_reduce, turned(image_inner_expand), image_inner_reduce),
        [(text_both, [text_qkv.shape[0], text_self_output.shape[0]])]
        + single(turned(image_self_weight), image_self_output),
        single(turned(text_outer_expand), text_outer_reduce, turned(image_outer_expand), image_outer_reduce),
    ]

    cross_jobs = [
        (0, 1, CO_DH, text_cross_output.shape[0] // CO_DH, 0),
        (1, 0, CO_DH, image_cross_output.shape[0] // CO_DH, 0),
    ]
    self_jobs = [
        (0, 0, TS_DH, text_self_output.shape[0] // TS_DH, 3 * text_self_output.shape[0]),
        (1, 1, VS_DH, image_self_output.shape[0] // VS_DH, 0),
    ]

    def rows_of(bias, gain, shift):
        return [jnp.stack([wide(bias[k]), gain[k], shift[k]]) for k in range(4)]

    text_rows = rows_of(text_branch_bias, text_gain, text_shift)
    image_rows = rows_of(image_branch_bias, image_gain, image_shift)
    if dp == 8:
        early_rows = [item for pair in zip(text_rows[:3], image_rows[:3]) for item in pair]
        gathered, bias_rows, early = gather(
            stages, bias_row, (text, image), early_rows, ids, (cross_jobs, self_jobs), places
        )
    else:
        gathered, bias_rows = gather_plain(stages, bias_row)
    text_cw, text_co, image_cw, image_co = gathered[:4]
    text_ie, text_ir, image_ie, image_ir = gathered[4:8]
    text_sb, image_sw, image_so = gathered[8:11]
    text_oe, text_or, image_oe, image_or = gathered[11:]
    bias_rows = jnp.concatenate([bias_row, bias_rows.reshape(tensor - 1, -1)], axis=0)
    offsets = [bias_rows[:, at : at + size].reshape(1, -1) for at, size in places]

    if dp == 8:
        text_cross, image_cross, text_inner, image_inner, text_self, image_self = early
    else:
        text_cross, image_cross = mix_forward(
            "cross",
            cross_jobs,
            ids,
            [
                (text, text_cw, text_co, offsets[0], text_rows[0]),
                (image, image_cw, image_co, offsets[1], image_rows[0]),
            ],
        )
        text_inner, image_inner = ffn_forward(
            "inner",
            [
                (text_cross[2], text_ie, text_ir, offsets[2], text_rows[1]),
                (image_cross[2], image_ie, image_ir, offsets[3], image_rows[1]),
            ],
        )
        text_self, image_self = mix_forward(
            "self",
            self_jobs,
            ids,
            [
                (text_inner[2], text_sb, text_sb, offsets[4], text_rows[2]),
                (image_inner[2], image_sw, image_so, offsets[5], image_rows[2]),
            ],
        )
    text_outer, image_outer = ffn_forward(
        "outer",
        [
            (text_self[2], text_oe, text_or, offsets[6], text_rows[3]),
            (image_self[2], image_oe, image_or, offsets[7], image_rows[3]),
        ],
    )
    text_result, image_result = text_outer[2], image_outer[2]

    text_part, image_part = text.shape[1] // dp, image.shape[1] // dp
    text_hidden, image_hidden = text_inner_offset.shape[0], image_inner_offset.shape[0]

    def ffn_reduction(states, backs, kepts):
        chunks = []
        for k in range(2):
            chunks += plain_chunks(text_part, k, text_hidden)
        for k in range(2):
            chunks += plain_chunks(image_part, 2 + k, image_hidden)
        lefts = [item for k in range(2) for item in (states[k], backs[k][1])]
        rights = [item for k in range(2) for item in (backs[k][3], kepts[k][1])]
        return chunks, lefts, rights

    def mix_reduction(states, backs, kepts, chunks):
        lefts = [item for k in range(2) for item in (states[k], backs[k][1])]
        rights = [item for k in range(2) for item in (backs[k][3], kepts[k][1])]
        return chunks, lefts, rights

    if dp == 8:
        qkv = 3 * text_self_output.shape[0]
        ffn_groups = [
            (text_part, text_hidden // LANES, [(0, text_hidden, 0)]),
            (text_part, text_hidden // LANES, [(1, text_hidden, 0)]),
            (image_part, image_hidden // LANES, [(2, image_hidden, 0)]),
            (image_part, image_hidden // LANES, [(3, image_hidden, 0)]),
        ]
        text_cols, image_cols = text_cross_output.shape[0], image_cross_output.shape[0]
        cross_groups = [
            (text_part, 3 * text_cols // LANES, [(0, 3 * text_cols, 0)]),
            (text_part, text_cols // LANES, [(1, text_cols, 0)]),
            (image_part, 3 * image_cols // LANES, [(2, 3 * image_cols, 0)]),
            (image_part, image_cols // LANES, [(3, image_cols, 0)]),
        ]
        both, plain_part = text_both.shape[0], qkv // LANES
        image_cols = image_self_output.shape[0]
        self_groups = [
            (text_part, plain_part, [(0, both, 0)]),
            (text_part, 1, [(0, both, plain_part * LANES), (1, both, plain_part * LANES)]),
            (image_part, 3 * image_cols // LANES, [(2, 3 * image_cols, 0)]),
            (image_part, image_cols // LANES, [(3, image_cols, 0)]),
        ]
        all_stages = [
            ("ffn", None, ((11, 12), (13, 14)), 3, ffn_groups),
            ("mix", self_jobs, ((8, 8), (9, 10)), 2, self_groups),
            ("ffn", None, ((4, 5), (6, 7)), 1, ffn_groups),
            ("mix", cross_jobs, ((0, 1), (2, 3)), 0, cross_groups),
        ]
        counts = [
            sum(count * repeat for count, repeat, _ in stage[4]) for stage in all_stages
        ]
        values = [(text_outer, image_outer), (text_self, image_self)]
        values += [(text_inner, image_inner), (text_cross, image_cross)]
        inputs = [(text_self[2], image_self[2]), (text_inner[2], image_inner[2])]
        inputs += [(text_cross[2], image_cross[2]), (wide(text), wide(image))]
        saved = []
        for pair, states in zip(values, inputs):
            for (columns, active, _, normed, scale), state in zip(pair, states):
                saved += [columns, normed, scale, active, state]
        back_rows = []
        for norm in (3, 2, 1, 0):
            back_rows += [text_rows[norm], image_rows[norm]]
        packed, (delta_text, delta_image), bias_sum, shared_sums = backward_all(
            all_stages,
            counts,
            places,
            [item.reshape(tensor, -1, item.shape[1]) for item in gathered],
            saved,
            (wide(text_cotangent), wide(image_cotangent)),
            back_rows,
            ids,
        )
    else:
        outer_back = ffn_backward(
            "outer_back",
            [
                (wide(text_cotangent), text_outer, text_oe, text_or, text_rows[3]),
                (wide(image_cotangent), image_outer, image_oe, image_or, image_rows[3]),
            ],
        )
        outer = ffn_reduction((text_self[2], image_self[2]), outer_back, (text_outer, image_outer))
        upstream = (outer_back[0][0], outer_back[1][0])

        self_back = mix_backward(
            "self_back",
            self_jobs,
            ids,
            [
                (upstream[0], text_self, text_sb, text_sb, text_rows[2]),
                (upstream[1], image_self, image_sw, image_so, image_rows[2]),
            ],
        )
        mixed_width = 3 * text_self_output.shape[0]
        chunks = []
        for at in range(0, text_both.shape[0], LANES):
            terms = [(0, 0, at)] if at < mixed_width else []
            if at + LANES > mixed_width:
                terms.append((1, 1, at))
            chunks.append((text_part, terms))
        chunks += plain_chunks(image_part, 2, 3 * image_self_output.shape[0])
        chunks += plain_chunks(image_part, 3, image_self_output.shape[0])
        own = mix_reduction((text_inner[2], image_inner[2]), self_back, (text_self, image_self), chunks)
        upstream = (self_back[0][0], self_back[1][0])

        inner_back = ffn_backward(
            "inner_back",
            [
                (upstream[0], text_inner, text_ie, text_ir, text_rows[1]),
                (upstream[1], image_inner, image_ie, image_ir, image_rows[1]),
            ],
        )
        inner = ffn_reduction((text_cross[2], image_cross[2]), inner_back, (text_inner, image_inner))
        upstream = (inner_back[0][0], inner_back[1][0])

        cross_back = mix_backward(
            "cross_back",
            cross_jobs,
            ids,
            [
                (upstream[0], text_cross, text_cw, text_co, text_rows[0]),
                (upstream[1], image_cross, image_cw, image_co, image_rows[0]),
            ],
        )
        delta_text, delta_image = cross_back[0][0], cross_back[1][0]
        chunks = plain_chunks(text_part, 0, 3 * text_cross_output.shape[0])
        chunks += plain_chunks(text_part, 1, text_cross_output.shape[0])
        chunks += plain_chunks(image_part, 2, 3 * image_cross_output.shape[0])
        chunks += plain_chunks(image_part, 3, image_cross_output.shape[0])
        cross = mix_reduction((text, image), cross_back, (text_cross, image_cross), chunks)
        backs = (cross_back, inner_back, self_back, outer_back)
        bias_deltas = (
            bias_parts(cross_back[0][4], text_cross_output.shape[0]),
            bias_parts(cross_back[1][4], image_cross_output.shape[0]),
            inner_back[0][4],
            inner_back[1][4],
            bias_parts(self_back[0][4], text_self_output.shape[0]),
            bias_parts(self_back[1][4], image_self_output.shape[0]),
            outer_back[0][4],
            outer_back[1][4],
        )
        by_near = jnp.concatenate([item.reshape(tensor, -1) for item in bias_deltas], axis=1)
        by_place = jnp.stack(
            [lax.dynamic_index_in_dim(by_near, place_t ^ s, 0, False) for s in range(tensor)]
        )
        shared = tuple(
            jnp.stack([back[k][2][kind] for back in backs]) for k in range(2) for kind in range(3)
        )
        line = jnp.concatenate([by_place.reshape(-1)] + [item.reshape(-1) for item in shared])
        line = line.reshape(-1, 128)
        packed = [reduce_plain(*item) for item in (outer, own, inner, cross)]
        line = lax.psum(line, ("dp", "tensor")).reshape(-1)
    text_wide, image_wide = text_cross_output.shape[0], image_cross_output.shape[0]
    text_own, image_own = text_self_output.shape[0], image_self_output.shape[0]
    ffn_layout = [
        (text_part, text_hidden // LANES, [("flat", text_hidden)]),
        (text_part, text_hidden // LANES, [("turn", text_hidden)]),
        (image_part, image_hidden // LANES, [("flat", image_hidden)]),
        (image_part, image_hidden // LANES, [("turn", image_hidden)]),
    ]
    own_layout = [
        (text_part, 4 * text_own // LANES, [("cube", 3 * text_own), ("turn", text_own)]),
        (image_part, 3 * image_own // LANES, [("cube", 3 * image_own)]),
        (image_part, image_own // LANES, [("turn", image_own)]),
    ]
    cross_layout = [
        (text_part, 3 * text_wide // LANES, [("cube", 3 * text_wide)]),
        (text_part, text_wide // LANES, [("turn", text_wide)]),
        (image_part, 3 * image_wide // LANES, [("cube", 3 * image_wide)]),
        (image_part, image_wide // LANES, [("turn", image_wide)]),
    ]
    layouts = [ffn_layout, own_layout, ffn_layout, cross_layout]
    deltas = unpack(packed, layouts)
    text_oe_delta, text_or_delta, image_oe_delta, image_or_delta = deltas[:4]
    text_sw_delta, text_so_delta, image_sw_delta, image_so_delta = deltas[4:8]
    text_ie_delta, text_ir_delta, image_ie_delta, image_ir_delta = deltas[8:12]
    text_cw_delta, text_co_delta, image_cw_delta, image_co_delta = deltas[12:]
    if dp == 8:
        pieces = [bias_sum[0, at : at + size] for at, size in places]
        bias_out = []
        for item, piece in zip(bias_order, pieces):
            if item.ndim == 2:
                width = item.shape[1]
                piece = jnp.stack([piece[:width], piece[2 * width : 3 * width]])
            bias_out.append(piece)
        shared_out = [value[:, kind] for value in shared_sums for kind in range(3)]
    else:
        by_place = lax.dynamic_index_in_dim(
            line[: by_place.size].reshape(by_place.shape), place_t, 0, False
        )
        bias_out, at = [], 0
        for item in bias_order:
            size = math.prod(item.shape)
            bias_out.append(by_place[at : at + size].reshape(item.shape))
            at += size
        shared_out, at = [], math.prod(by_near.shape)
        for item in shared:
            shared_out.append(line[at : at + item.size].reshape(item.shape))
            at += item.size

    return (
        text_result,
        image_result,
        delta_text,
        delta_image,
        text_cw_delta,
        bias_out[0],
        text_co_delta,
        text_ie_delta,
        bias_out[2],
        text_ir_delta,
        text_sw_delta,
        bias_out[4],
        text_so_delta,
        text_oe_delta,
        bias_out[6],
        text_or_delta,
        shared_out[0],
        shared_out[1],
        shared_out[2],
        image_cw_delta,
        bias_out[1],
        image_co_delta,
        image_ie_delta,
        bias_out[3],
        image_ir_delta,
        image_sw_delta,
        bias_out[5],
        image_so_delta,
        image_oe_delta,
        bias_out[7],
        image_or_delta,
        shared_out[3],
        shared_out[4],
        shared_out[5],
    )


def solution(mesh):
    placed = (
        P(("dp", "tensor"), None),
        P(("dp", "tensor"), None),
        P("dp", None),
        P("dp", None),
        P(None, None, "tensor"),
        P(None, "tensor"),
        P("tensor", None),
        P(None, "tensor"),
        P("tensor"),
        P("tensor", None),
        P(None, None, "tensor"),
        P(None, "tensor"),
        P("tensor", None),
        P(None, "tensor"),
        P("tensor"),
        P("tensor", None),
        P(),
        P(),
        P(),
        P(None, None, "tensor"),
        P(None, "tensor"),
        P("tensor", None),
        P(None, "tensor"),
        P("tensor"),
        P("tensor", None),
        P(None, None, "tensor"),
        P(None, "tensor"),
        P("tensor", None),
        P(None, "tensor"),
        P("tensor"),
        P("tensor", None),
        P(),
        P(),
        P(),
        P(("dp", "tensor"), None),
        P(("dp", "tensor"), None),
    )
    return jax.shard_map(
        per_device,
        mesh=mesh,
        in_specs=placed,
        out_specs=(
            P(("dp", "tensor"), None),
            P(("dp", "tensor"), None),
            P(("dp", "tensor"), None),
            P(("dp", "tensor"), None),
            P("dp", None, "tensor"),
            P(None, "tensor"),
            P("tensor", "dp"),
            P("dp", "tensor"),
            P("tensor"),
            P("tensor", "dp"),
            P("dp", None, "tensor"),
            P(None, "tensor"),
            P("tensor", "dp"),
            P("dp", "tensor"),
            P("tensor"),
            P("tensor", "dp"),
            P(),
            P(),
            P(),
            P("dp", None, "tensor"),
            P(None, "tensor"),
            P("tensor", "dp"),
            P("dp", "tensor"),
            P("tensor"),
            P("tensor", "dp"),
            P("dp", None, "tensor"),
            P(None, "tensor"),
            P("tensor", "dp"),
            P("dp", "tensor"),
            P("tensor"),
            P("tensor", "dp"),
            P(),
            P(),
            P(),
        ),
        check_vma=False,
    )
```

profile of v0, /device:TPU:0, one launch (start us, length us, event | category | flops | bytes accessed | tf_op | source)
XLA Modules:
  0.0 584.7 jit_solution(16041671214733463217)
XLA Ops:
  0.7 2.5 copy.80
  3.2 1.7 copy.81
  4.9 1.5 copy.82
  6.4 1.0 copy.83
  7.4 2.4 pad_maximum_fusion.refs_8_
  9.8 1.7 copy.84
  11.5 0.0 copy-start.24
  11.6 0.0 copy-start.28
  11.6 0.0 copy-start.29
  11.7 1.5 copy.85
  13.2 1.0 copy.86
  14.3 0.1 concatenate.10
  14.4 0.6 reshape.141.refs_15_
  15.1 0.6 pad_maximum_fusion.5
  15.8 0.6 pad_maximum_fusion.1
  16.5 0.6 pad_maximum_fusion.7
  17.1 0.6 pad_maximum_fusion.3
  17.7 0.8 dynamic-slice_add_fusion.1
  18.5 0.8 copy.87.refs_24_.refs_65_
  19.3 0.8 dynamic-slice_add_fusion
  20.0 0.7 reshape.153.refs_26_.refs_67_
  20.8 0.6 reshape.145.refs_27_.refs_68_
  21.4 220.3 %gather.1 = (bf16[4,768,768]{2,1,0:T(8,128)(2,1)}, bf16[4,256,768]{2,1,0:T(8,128)(2,1)}, bf16[4,768,1024]{2,1,0:T(8,128)(2,1)}, bf16[4,256,1024]{2,1,0:T(8,128)(...) custom-call(bf16[768,768]{1,0:T(8,128)(2,1)} %bitcast.67, ...), custom_call_target="tpu_custom_call" | custom-call | tf_op jit(solution)/shard_map/gather/pallas_call | solution.py:272
  241.7 0.9 copy.108
  242.6 0.6 copy.99
  243.2 0.6 copy.100
  243.8 13.0 %outer.1 = (f32[256,3072]{1,0:T(8,128)}, bf16[256,3072]{1,0:T(8,128)(2,1)}, f32[256,768]{1,0:T(8,128)}, f32[256,768]{1,0:T(8,128)}, f32[256,128]{1,0:T(8,128)}, ...) custom-call(f32[256,768]{1,0:T(8,128)} %get-tuple-element.115.refs_0, ...), custom_call_target="tpu_custom_call" | custom-call | tf_op jit(solution)/shard_map/outer/pallas_call | solution.py:1042
  256.9 1.0 convert_element_type.68.refs_49_
  257.9 0.7 convert_element_type.69.refs_54_
  258.6 1.0 convert_element_type.70.refs_55_
  259.6 0.7 convert_element_type.71.refs_56_
  260.3 309.4 %backward.1 = (f32[832,256]{1,0:T(8,128)}, f32[800,256]{1,0:T(8,128)}, f32[832,256]{1,0:T(8,128)}, f32[896,256]{1,0:T(8,128)}, f32[256,768]{1,0:T(8,128)}, /*ind...) custom-call(bf16[4,768,768]{2,1,0:T(8,128)(2,1)} %get-tuple-element., ...), custom_call_target="tpu_custom_call" | custom-call | tf_op jit(solution)/shard_map/backward/pallas_call | solution.py:754
  569.8 4.0 unpack.1
  573.7 0.6 fusion.3
  574.3 0.6 pad_maximum_fusion.10
  574.9 0.6 slice_reduce_fusion
  575.5 0.6 pad_maximum_fusion.11
  576.1 1.6 copy.91
  577.8 0.6 copy.114
  578.4 0.6 copy.113
  579.0 0.6 copy.112
  579.6 0.6 pad_maximum_fusion.12
  580.2 0.6 pad_maximum_fusion.13
  580.8 0.6 copy.111
  581.4 0.6 copy.110
  582.0 0.6 copy.109
  582.6 0.9 copy.117
  583.5 0.7 copy.118
  (76 shorter events, 0.4 us)
Async XLA Ops:
  0.7 2.5 copy-start
  3.2 1.8 copy-start.3
  4.9 1.5 copy-start.7
  6.4 3.4 copy-start.1
  9.8 1.7 copy-start.4
  11.5 1.6 copy-start.8
  11.5 2.6 copy-start.25
  11.5 2.7 copy-start.23
  11.5 2.7 copy-start.24
  11.6 2.7 copy-start.26
  11.6 2.7 copy-start.27
  11.6 2.7 copy-start.28
  11.6 2.7 copy-start.29
  11.6 2.7 copy-start.30
  11.6 3.4 copy-start.18
  11.6 3.4 copy-start.19
  11.6 3.5 copy-start.20
  11.7 4.1 copy-start.14
  11.7 4.1 copy-start.15
  11.7 4.1 copy-start.16
  18.5 2.9 copy-start.21
  21.4 221.2 %copy-start.10 = (bf16[1,5120]{1,0:T(2,128)(2,1)S(1)}, bf16[1,5120]{1,0:T(2,128)(2,1)}, u32[]{:S(2)}) copy-start(bf16[1,5120]{1,0:T(2,128)(2,1)} %reshape.141.refs_15_) | copy-start | bytes 30724
  243.8 13.0 %copy-start.2 = (bf16[256,768]{1,0:T(8,128)(2,1)S(1)}, bf16[256,768]{1,0:T(8,128)(2,1)}, u32[]{:S(2)}) copy-start(bf16[256,768]{1,0:T(8,128)(2,1)} %refs_16_.1) | copy-start | bytes 1179652
  243.8 14.0 %copy-start.6 = (bf16[72,1024]{1,0:T(8,128)(2,1)S(1)}, bf16[72,1024]{1,0:T(8,128)(2,1)}, u32[]{:S(2)}) copy-start(bf16[72,1024]{1,0:T(8,128)(2,1)} %refs_17_.1) | copy-start | bytes 442372
  256.8 1.8 copy-start.9
  256.9 2.7 copy-start.12
  569.7 4.0 copy-start.22
  569.7 8.0 %copy-start.17 = (f32[4,3,768]{2,1,0:T(4,128)S(1)}, f32[4,3,768]{2,1,0:T(4,128)}, u32[]{:S(2)}) copy-start(f32[4,3,768]{2,1,0:T(4,128)} %get-tuple-element.186) | copy-start | bytes 110596
  569.8 11.0 %copy-start.13 = (f32[4,3,1024]{2,1,0:T(4,128)S(1)}, f32[4,3,1024]{2,1,0:T(4,128)}, u32[]{:S(2)}) copy-start(f32[4,3,1024]{2,1,0:T(4,128)} %get-tuple-element.195) | copy-start | bytes 147460
  569.8 12.9 %copy-start.5 = (f32[256,768]{1,0:T(8,128)S(1)}, f32[256,768]{1,0:T(8,128)}, u32[]{:S(2)}) copy-start(f32[256,768]{1,0:T(8,128)} %get-tuple-element.360) | copy-start | bytes 2359300
  573.7 9.8 %copy-start.11 = (f32[72,1024]{1,0:T(8,128)S(1)}, f32[72,1024]{1,0:T(8,128)}, u32[]{:S(2)}) copy-start(f32[72,1024]{1,0:T(8,128)} %get-tuple-element.361) | copy-start | bytes 884740
where the time goes:
time: 596 us; the launch traced here: 585 us
  Pallas kernels  547 us (92%)
  local copies, waits for them, and re-layouts  24.2 us (4%)
  other arithmetic  12.2 us (2%)
    pallas_call x1, Pallas kernels, backward_all(): pl.pallas_call(functools.partial(backward_kernel, stages, counts, places,...  309 us
    pallas_call x1, Pallas kernels, gather(): pl.pallas_call(functools.partial(gather_kernel, segments, stage_of, len(m...  220 us
    unnamed x81, local copies, waits for them, and re-layouts  20 us
    pallas_call x1, Pallas kernels, run_stage(): pl.pallas_call(functools.partial(stage_kernel, body, jobs, len(ids), len(...  13 us

commit v1 on v0

--- a/solution.py
+++ b/solution.py
@@ -647,6 +647,10 @@
         following = step // 2 + 1 if step % 2 == 0 and step // 2 + 1 < n else None
         if step < len(pairs):
             square(step)
+            if step % 2 and step + 1 < len(pairs):
+                back(step // 2 + 1, 3)
+                if step // 2 + 1 == n - 1:
+                    delta_moves += [move(upstream[k], deltas[k]) for k in range(2)]
             if step + 1 < len(pairs):
                 produce(step + 1)
         if following is not None:
@@ -659,10 +663,6 @@
             back(following, 2)
         if 0 <= step - 2 < len(pairs):
             line(step - 2)
-        if following is not None:
-            back(following, 3)
-        if following == n - 1:
-            delta_moves += [move(upstream[k], deltas[k]) for k in range(2)]
         if step >= 3 and (step - 3) % 2:
             finish_stage((step - 3) // 2)
         if 0 <= step - 5 <= 5:
@@ -782,10 +782,19 @@
     return found
 
 
-def unpack_kernel(layouts, *refs):
+def unpack_kernel(layouts, smalls, *refs):
     n = len(layouts)
     n_out = sum(len(parts) for layout in layouts for _, _, parts in layout)
-    packed, outs, line = refs[:n], refs[n : n + n_out], refs[n + n_out]
+    packed, (bias_sum, *shared), refs = refs[:n], refs[n : n + 3], refs[n + 3 :]
+    outs, small_outs, line = refs[:n_out], refs[n_out:-1], refs[-1]
+    for out, (at, _, paired) in zip(small_outs, smalls):
+        width = out.shape[1]
+        out[0:1, :] = bias_sum[:, at : at + width]
+        if paired:
+            out[1:2, :] = bias_sum[:, at + 2 * width : at + 3 * width]
+    for index, out in enumerate(small_outs[len(smalls) :]):
+        for k in range(4):
+            out[k : k + 1, :] = shared[index // 3][k, index % 3 : index % 3 + 1, :]
     index = 0
     for source, layout in zip(packed, layouts):
         at = 0
@@ -809,7 +818,7 @@
                 first += columns
 
 
-def unpack(packed, layouts):
+def unpack(packed, layouts, smalls=(), sums=()):
     if lax.axis_size("dp") != 8:
         return [item for value, layout in zip(packed, layouts) for item in split_packed(value, layout)]
     shapes, top, widest = [], 0, 0
@@ -825,18 +834,23 @@
                     }[kind]
                 )
     found = pl.pallas_call(
-        functools.partial(unpack_kernel, layouts),
-        out_shape=[jax.ShapeDtypeStruct(shape, f32) for shape in shapes],
+        functools.partial(unpack_kernel, layouts, smalls),
+        out_shape=[
+            jax.ShapeDtypeStruct(shape, f32)
+            for shape in shapes
+            + [(2 if paired else 1, width) for _, width, paired in smalls]
+            + [(4, value.shape[2]) for value in sums[1:] for _ in range(3)]
+        ],
         scratch_shapes=[pltpu.VMEM((top, widest), f32)],
         name="unpack",
-    )(*packed)
+    )(*packed, *sums)
     kinds = [(kind, rows) for layout in layouts for rows, _, parts in layout for kind, _ in parts]
     return [
         item.transpose(1, 0, 2)
         if kind == "cube"
         else (item.T if kind == "turn" and rows % 128 else item)
         for item, (kind, rows) in zip(found, kinds)
-    ]
+    ] + list(found[len(kinds) :])
 
 
 def row_sum(value):
@@ -1464,20 +1478,20 @@
         (image_part, image_wide // LANES, [("turn", image_wide)]),
     ]
     layouts = [ffn_layout, own_layout, ffn_layout, cross_layout]
-    deltas = unpack(packed, layouts)
+    if dp == 8:
+        smalls = [
+            (at, item.shape[-1], item.ndim == 2) for item, (at, _) in zip(bias_order, places)
+        ]
+        deltas = unpack(packed, layouts, smalls, (bias_sum, *shared_sums))
+    else:
+        deltas = unpack(packed, layouts)
     text_oe_delta, text_or_delta, image_oe_delta, image_or_delta = deltas[:4]
     text_sw_delta, text_so_delta, image_sw_delta, image_so_delta = deltas[4:8]
     text_ie_delta, text_ir_delta, image_ie_delta, image_ir_delta = deltas[8:12]
-    text_cw_delta, text_co_delta, image_cw_delta, image_co_delta = deltas[12:]
+    text_cw_delta, text_co_delta, image_cw_delta, image_co_delta = deltas[12:16]
     if dp == 8:
-        pieces = [bias_sum[0, at : at + size] for at, size in places]
-        bias_out = []
-        for item, piece in zip(bias_order, pieces):
-            if item.ndim == 2:
-                width = item.shape[1]
-                piece = jnp.stack([piece[:width], piece[2 * width : 3 * width]])
-            bias_out.append(piece)
-        shared_out = [value[:, kind] for value in shared_sums for kind in range(3)]
+        bias_out = [value.reshape(item.shape) for value, item in zip(deltas[16:24], bias_order)]
+        shared_out = deltas[24:]
     else:
         by_place = lax.dynamic_index_in_dim(
             line[: by_place.size].reshape(by_place.shape), place_t, 0, False

time: 596 us -> 586 us (0.983)
  Pallas kernels: 547 us -> 541 us
    unnamed x81 -> x69, local copies, waits for them, and re-layouts: 20 us -> 16.4 us
where the time goes in v1:
time: 586 us; the launch traced here: 574 us
  Pallas kernels  541 us (92%)
  local copies, waits for them, and re-layouts  19.4 us (3%)
  other arithmetic  12.5 us (2%)
    pallas_call x1, Pallas kernels, backward_all(): pl.pallas_call(functools.partial(backward_kernel, stages, counts, places,...  304 us
    pallas_call x1, Pallas kernels, gather(): pl.pallas_call(functools.partial(gather_kernel, segments, stage_of, len(m...  220 us
    unnamed x69, local copies, waits for them, and re-layouts  16.4 us
    pallas_call x1, Pallas kernels, run_stage(): pl.pallas_call(functools.partial(stage_kernel, body, jobs, len(ids), len(...  13 us

profile of v1, /device:TPU:0, one launch (start us, length us, event | category | flops | bytes accessed | tf_op | source)
XLA Modules:
  0.0 574.4 jit_solution(950541683921870469)
XLA Ops:
  0.7 2.5 copy.80
  3.2 1.7 copy.81
  5.0 1.5 copy.82
  6.4 1.0 copy.83
  7.5 2.4 pad_maximum_fusion.refs_8_
  9.8 1.8 copy.84
  11.6 0.0 copy-start.21
  11.6 0.0 copy-start.23
  11.6 0.0 copy-start.24
  11.6 0.0 copy-start.25
  11.6 0.0 copy-start.26
  11.6 0.0 copy-start.27
  11.6 0.0 copy-start.16
  11.7 0.0 copy-start.17
  11.7 0.0 copy-start.18
  11.7 0.0 copy-start.13
  11.7 0.0 copy-start.14
  11.7 0.0 copy-start.15
  11.7 1.5 copy.85
  13.2 1.0 copy.86
  14.4 0.1 concatenate.10
  14.5 0.6 reshape.137.refs_15_
  15.2 0.6 pad_maximum_fusion.5
  15.9 0.6 pad_maximum_fusion.1
  16.5 0.6 pad_maximum_fusion.7
  17.1 0.6 pad_maximum_fusion.3
  17.8 0.8 dynamic-slice_add_fusion.1
  18.5 0.8 copy.87.refs_24_.refs_65_
  19.3 0.8 dynamic-slice_add_fusion
  20.1 0.7 reshape.153.refs_26_.refs_67_
  20.8 0.6 reshape.141.refs_27_.refs_68_
  21.4 220.3 %gather.1 = (bf16[4,768,768]{2,1,0:T(8,128)(2,1)}, bf16[4,256,768]{2,1,0:T(8,128)(2,1)}, bf16[4,768,1024]{2,1,0:T(8,128)(2,1)}, bf16[4,256,1024]{2,1,0:T(8,128)(...) custom-call(bf16[768,768]{1,0:T(8,128)(2,1)} %bitcast.49, ...), custom_call_target="tpu_custom_call" | custom-call | tf_op jit(solution)/shard_map/gather/pallas_call | solution.py:272
  241.7 0.9 copy.96
  242.6 0.6 copy.93
  243.3 0.6 copy.94
  243.9 13.0 %outer.1 = (f32[256,3072]{1,0:T(8,128)}, bf16[256,3072]{1,0:T(8,128)(2,1)}, f32[256,768]{1,0:T(8,128)}, f32[256,768]{1,0:T(8,128)}, f32[256,128]{1,0:T(8,128)}, ...) custom-call(f32[256,768]{1,0:T(8,128)} %get-tuple-element.129.refs_0, ...), custom_call_target="tpu_custom_call" | custom-call | tf_op jit(solution)/shard_map/outer/pallas_call | solution.py:1056
  256.9 0.0 copy-start.9
  256.9 1.0 convert_element_type.68.refs_49_
  257.9 0.7 convert_element_type.69.refs_54_
  258.6 1.0 convert_element_type.70.refs_55_
  259.6 0.7 convert_element_type.71.refs_56_
  260.3 303.8 %backward.1 = (f32[832,256]{1,0:T(8,128)}, f32[800,256]{1,0:T(8,128)}, f32[832,256]{1,0:T(8,128)}, f32[896,256]{1,0:T(8,128)}, f32[256,768]{1,0:T(8,128)}, /*ind...) custom-call(bf16[4,768,768]{2,1,0:T(8,128)(2,1)} %get-tuple-element., ...), custom_call_target="tpu_custom_call" | custom-call | tf_op jit(solution)/shard_map/backward/pallas_call | solution.py:754
  564.1 4.0 unpack.1
  568.2 1.3 reduce.8
  569.5 1.6 copy.91
  571.1 1.3 reduce.9
  572.4 0.9 copy.99
  573.3 0.7 copy.100
  (57 shorter events, 0.3 us)
Async XLA Ops:
  0.7 2.5 copy-start
  3.2 1.8 copy-start.3
  5.0 1.5 copy-start.7
  6.4 3.4 copy-start.1
  9.8 1.8 copy-start.4
  11.6 1.6 copy-start.8
  11.6 2.6 copy-start.22
  11.6 2.7 copy-start.20
  11.6 2.7 copy-start.21
  11.6 2.7 copy-start.23
  11.6 2.7 copy-start.24
  11.6 2.7 copy-start.25
  11.6 2.7 copy-start.26
  11.6 2.7 copy-start.27
  11.6 3.4 copy-start.16
  11.7 3.4 copy-start.17
  11.7 3.5 copy-start.18
  11.7 4.1 copy-start.13
  11.7 4.1 copy-start.14
  11.7 4.1 copy-start.15
  18.5 2.9 copy-start.19
  21.4 221.2 %copy-start.10 = (bf16[1,5120]{1,0:T(2,128)(2,1)S(1)}, bf16[1,5120]{1,0:T(2,128)(2,1)}, u32[]{:S(2)}) copy-start(bf16[1,5120]{1,0:T(2,128)(2,1)} %reshape.137.refs_15_) | copy-start | bytes 30724
  243.9 13.1 %copy-start.2 = (bf16[256,768]{1,0:T(8,128)(2,1)S(1)}, bf16[256,768]{1,0:T(8,128)(2,1)}, u32[]{:S(2)}) copy-start(bf16[256,768]{1,0:T(8,128)(2,1)} %refs_16_.1) | copy-start | bytes 1179652
  243.9 14.0 %copy-start.6 = (bf16[72,1024]{1,0:T(8,128)(2,1)S(1)}, bf16[72,1024]{1,0:T(8,128)(2,1)}, u32[]{:S(2)}) copy-start(bf16[72,1024]{1,0:T(8,128)(2,1)} %refs_17_.1) | copy-start | bytes 442372
  256.9 1.7 copy-start.9
  256.9 2.7 copy-start.12
  564.1 8.3 %copy-start.5 = (f32[256,768]{1,0:T(8,128)S(1)}, f32[256,768]{1,0:T(8,128)}, u32[]{:S(2)}) copy-start(f32[256,768]{1,0:T(8,128)} %get-tuple-element.370) | copy-start | bytes 2359300
  568.1 5.1 copy-start.11
